TPU v7x, 32 devices: a whole 2x2x4 slice. The times are simulated.
32 devices in a mesh: chan: 4 (over y, core), prof: 8 (over z, x).
Axes of the slice: x: 2, y: 2, z: 4, core: 2. Of those that a mesh axis runs over, the one named last changes fastest.
Arguments:
- observed: bfloat16 [32, 8448], P('prof', 'chan'), may hold values from -6 to 6
- eigvec: bfloat16 [8448, 300], P('chan'), may hold values from -0.0625 to 0.0625
- jacobian: bfloat16 [32, 8448, 400], P('prof', 'chan'), may hold values from -0.44921875 to 0.44921875
- radiance_base: bfloat16 [8448], P('chan'), may hold values from -1 to 1
- curvature: bfloat16 [8448], P('chan'), may hold values from -0.29882812 to 0.29882812
- block_mask: int32 [32, 256], P('prof', 'chan'), may hold values 0 or 1
- pc_weight: float32 [300], replicated, may hold values from 0.2 to 2
- prior_prec: float32 [400], replicated, may hold values from 0.3 to 3
- prior_mean: float32 [32, 400], P(('prof', 'chan')), may hold values from -6 to 6
- state0: float32 [32, 400], P(('prof', 'chan')), may hold values from -6 to 6
Outputs:
- states: float32 [32, 400], P(('prof', 'chan'))
All inputs are finite; a program needn't handle non-finite values. No bound on the sum of `block_mask` on one device may be relied on, other than what follows from the above.
Results may differ from a plain program's by a relative error of at most 0.006.
Values may be sent and summed in bfloat16 or wider, within the bound.
A program may use at most 128 MiB of HBM per device.

v0:
```python
import jax
import jax.numpy as jnp
from jax import lax
from jax.sharding import PartitionSpec as P

ITERS = 2


def solve_step(states, pc_resid, pc_jacob, pc_weight, prior_prec, prior_mean):
    highest = lax.Precision.HIGHEST
    weighted_jac = pc_jacob * pc_weight[None, :, None]
    normal = jnp.einsum("rks,rkt->rst", weighted_jac, pc_jacob, precision=highest)
    normal = (
        normal + jnp.eye(pc_jacob.shape[2], dtype=jnp.float32)[None] * prior_prec[None, None, :]
    )
    gradient = jnp.einsum("rks,rk->rs", pc_jacob, pc_weight[None, :] * pc_resid, precision=highest)
    gradient = gradient + prior_prec[None, :] * (states - prior_mean)
    factor = jnp.linalg.cholesky(normal)

    def one_solve(fac, vec):
        return jax.scipy.linalg.cho_solve((fac, True), vec)

    update = jax.vmap(one_solve)(factor, gradient)
    return states - update


def project(state_bf, spectra, valid, eigvec, jacobian, radiance_base, curvature):
    shift_f = radiance_base.astype(jnp.float32)
    curve_f = curvature.astype(jnp.float32)
    linear = jnp.einsum("rs,rcs->rc", state_bf, jacobian, preferred_element_type=jnp.float32)
    misfit = (
        valid * (shift_f + linear + 0.5 * curve_f * linear * linear - spectra.astype(jnp.float32))
    ).astype(jnp.bfloat16)
    slope = valid * (1.0 + curve_f * linear)
    weighted = (slope[:, :, None] * eigvec[None]).astype(jnp.bfloat16)
    pc_resid = jnp.dot(misfit, eigvec, preferred_element_type=jnp.float32)
    pc_jacob = jnp.einsum("rck,rcs->rks", weighted, jacobian, preferred_element_type=jnp.float32)
    return (pc_resid, pc_jacob)


def local(
    observed,
    eigvec,
    jacobian,
    radiance_base,
    curvature,
    block_mask,
    pc_weight,
    prior_prec,
    prior_mean,
    state0,
):
    block_width = observed.shape[1] // block_mask.shape[1]
    states = state0
    valid = jnp.repeat(block_mask.astype(jnp.float32), block_width, axis=1)
    for iteration in range(ITERS):
        state_bf = lax.all_gather(states.astype(jnp.bfloat16), "chan", axis=0, tiled=True)
        pc_resid, pc_jacob = project(
            state_bf, observed, valid, eigvec, jacobian, radiance_base, curvature
        )
        pc_resid, pc_jacob = (
            lax.psum_scatter(pc_resid, "chan", scatter_dimension=0, tiled=True),
            lax.psum_scatter(pc_jacob, "chan", scatter_dimension=0, tiled=True),
        )
        states = solve_step(states, pc_resid, pc_jacob, pc_weight, prior_prec, prior_mean)
    return states


def solution(mesh):
    return jax.shard_map(
        local,
        mesh=mesh,
        in_specs=(
            P("prof", "chan"),
            P("chan", None),
            P("prof", "chan", None),
            P("chan"),
            P("chan"),
            P("prof", "chan"),
            P(),
            P(),
            P(("prof", "chan"), None),
            P(("prof", "chan"), None),
        ),
        out_specs=P(("prof", "chan"), None),
        check_vma=False,
    )
```

profile of v0, /device:TPU:0, one launch (start us, length us, event | category | flops | bytes accessed | tf_op | source)
XLA Modules:
  0.0 412.0 jit_solution(6302252170544993609)
XLA Ops:
  8.2 6.2 %all-gather = bf16[4,1,400]{2,1,0:T(2,128)(2,1)S(1)} all-gather(bf16[1,1,400]{2,1,0:T(2,128)(2,1)S(1)} %convert_bitcast_fusion.2), channel_id=1, replica_groups=mesh['chan'=4,'prof'=8] {'chan'}, dimensions={0}, use_global_device_ids=true | all-gather | bytes 4000 | tf_op jit(solution)/shard_map/all_gather | solution.py:57
  16.7 5.3 %fusion.90 = f32[4,1,2112]{2,1,0:T(1,128)S(1)} fusion(bf16[4,2112,400]{1,2,0:T(8,128)(2,1)} %param.15, bf16[4,1,400]{2,1,0:T(2,128)(2,1)S(1)} %all-gather), kind=kOutput, calls=%fused_computation.197 | convolution fusion | flops 6758400 | bytes 6795392 | tf_op jit(solution)/shard_map/rs,rcs->rc/dot_general | solution.py:30
  22.1 5.4 %fusion = f32[4,300,400]{1,2,0:T(8,128)} fusion(bf16[4,2112,400]{1,2,0:T(8,128)(2,1)S(1)} %copy-done, f32[2112,300]{0,1:T(8,128)S(1)} %convert_element_type.43, f32[4,2112]{1,0:T(4,128)S(1)} %fusion.79), kind=kOutput, calls=%fused_computation.6 | convolution fusion | flops 2032588800 | bytes 11246592 | tf_op jit(solution)/shard_map/rck,rcs->rks/dot_general | solution.py:37
  29.4 8.3 %all-reduce.3 = f32[4,300]{1,0:T(4,128)} all-reduce(f32[4,300]{1,0:T(4,128)S(1)} %fusion.82), channel_id=3, replica_groups=mesh['chan'=4,'prof'=8] {'chan'}, use_global_device_ids=true, to_apply=%region_9.11.clone | all-reduce | flops 1200 | bytes 9600
  38.2 24.7 %reduce-scatter.3.cloned.1.call-done = f32[1,300,400]{1,2,0:T(8,128)} async-done(((f32[4,300,400]{1,2,0:T(8,128)}), f32[1,300,400]{1,2,0:T(8,128)}) %reduce-scatter.3.cloned.1.call-update) | async-done | bytes 480016 | tf_op jit(solution)/shard_map/reduce_scatter | solution.py:63
  62.9 2.7 convolution_add_fusion.1
  66.2 11.7 %custom-call.37 = f32[1,128,128]{2,1,0:T(8,128)S(1)} custom-call(f32[1,128,128]{2,1,0:T(8,128)S(1)} %cholesky.439), custom_call_target="Cholesky" | custom-call | tf_op jit(solution)/shard_map/jit(cholesky)/cholesky | solution.py:18
  78.4 10.4 %custom-call.38 = f32[1,1,128,128]{2,3,1,0:T(8,128)} custom-call(f32[1,1,128,128]{3,2,1,0:T(8,128)S(1)} %get-tuple-element.60), custom_call_target="InvertDiagBlocksLowerTriangular" | custom-call | tf_op jit(solution)/shard_map/jit(cholesky)/cholesky | solution.py:18
  94.3 12.9 %custom-call.39 = f32[1,128,128]{2,1,0:T(8,128)S(1)} custom-call(f32[1,128,128]{2,1,0:T(8,128)} %cholesky.443), custom_call_target="Cholesky" | custom-call | tf_op jit(solution)/shard_map/jit(cholesky)/cholesky | solution.py:18
  108.5 10.6 %custom-call.40 = f32[1,1,128,128]{2,3,1,0:T(8,128)S(1)} custom-call(f32[1,1,128,128]{3,2,1,0:T(8,128)} %get-tuple-element.57), custom_call_target="InvertDiagBlocksLowerTriangular" | custom-call | tf_op jit(solution)/shard_map/jit(cholesky)/cholesky | solution.py:18
  122.8 12.3 %custom-call.41 = f32[1,128,128]{2,1,0:T(8,128)} custom-call(f32[1,128,128]{2,1,0:T(8,128)S(1)} %cholesky.448), custom_call_target="Cholesky" | custom-call | tf_op jit(solution)/shard_map/jit(cholesky)/cholesky | solution.py:18
  137.2 10.4 %custom-call.42 = f32[1,1,128,128]{2,3,1,0:T(8,128)} custom-call(f32[1,1,128,128]{3,2,1,0:T(8,128)S(1)} %get-tuple-element.54), custom_call_target="InvertDiagBlocksLowerTriangular" | custom-call | tf_op jit(solution)/shard_map/jit(cholesky)/cholesky | solution.py:18
  159.4 10.6 %while.4 = (s32[]{:T(128)}, f32[1,400,400]{2,1,0:T(8,128)}, s32[3,2]{0,1:T(2,128)S(1)}, f32[3,1,128,128]{3,2,1,0:T(8,128)}, s32[]{:T(128)}) while((s32[]{:T(128)}, f32[1,400,400]{2,1,0:T(8,128)}, s32[3,2]{0,1:T(2,128)S(1)}, f32[3,1,128,128]{3,2,1,0:T(8,128)}, s32[]{:T(128)}) %tuple.62), condition=%wide.while_cond, body=%wide.while_body.sunk | while | flops 2 | bytes 132705 | solution.py:21
  160.1 2.9 bitcast_dynamic-update-slice_fusion.4
  163.6 2.9 bitcast_dynamic-update-slice_fusion.4
  167.1 2.9 bitcast_dynamic-update-slice_fusion.4
  171.7 40.7 %custom-call.44 = f32[1,4,128,128]{2,3,1,0:T(8,128)} custom-call(f32[1,4,128,128]{3,2,1,0:T(8,128)} %pad_maximum_fusion), custom_call_target="InvertDiagBlocksLowerTriangular" | custom-call | tf_op jit(solution)/shard_map/vmap(jit(_cho_solve))/triangular_solve | solution.py:21
  212.5 2.2 fusion.17
  229.6 5.2 %all-gather.1 = bf16[4,1,400]{2,1,0:T(2,128)(2,1)S(1)} all-gather(bf16[1,1,400]{2,1,0:T(2,128)(2,1)S(1)} %get-tuple-element.39), channel_id=1, replica_groups=mesh['chan'=4,'prof'=8] {'chan'}, dimensions={0}, use_global_device_ids=true | all-gather | bytes 4000 | tf_op jit(solution)/shard_map/all_gather | solution.py:57
  234.8 4.0 fusion.88
  238.9 5.5 %fusion.1 = f32[4,300,400]{1,2,0:T(8,128)} fusion(bf16[4,2112,400]{1,2,0:T(8,128)(2,1)S(1)} %bitcast.561, f32[4,2112]{1,0:T(4,128)S(1)} %fusion.77, f32[2112,300]{0,1:T(8,128)S(1)} %copy-done.6), kind=kOutput, calls=%fused_computation.7 | convolution fusion | flops 2032588800 | bytes 11246592 | tf_op jit(solution)/shard_map/rck,rcs->rks/dot_general | solution.py:37
  246.2 6.3 %all-reduce.4 = f32[4,300]{1,0:T(4,128)S(1)} all-reduce(f32[4,300]{1,0:T(4,128)S(1)} %fusion.80), channel_id=5, replica_groups=mesh['chan'=4,'prof'=8] {'chan'}, use_global_device_ids=true, to_apply=%region_11.14.clone | all-reduce | flops 1200 | bytes 9600
  252.5 25.5 %reduce-scatter.5.cloned.1.call-done = f32[1,300,400]{1,2,0:T(8,128)} async-done(((f32[4,300,400]{1,2,0:T(8,128)}), f32[1,300,400]{1,2,0:T(8,128)}) %reduce-scatter.5.cloned.1.call-update) | async-done | bytes 480016 | tf_op jit(solution)/shard_map/reduce_scatter | solution.py:63
  278.0 2.7 convolution_add_fusion
  281.2 11.7 %custom-call.45 = f32[1,128,128]{2,1,0:T(8,128)S(1)} custom-call(f32[1,128,128]{2,1,0:T(8,128)S(1)} %cholesky.452), custom_call_target="Cholesky" | custom-call | tf_op jit(solution)/shard_map/jit(cholesky)/cholesky | solution.py:18
  293.1 9.8 %custom-call.46 = f32[1,1,128,128]{2,3,1,0:T(8,128)S(1)} custom-call(f32[1,1,128,128]{3,2,1,0:T(8,128)S(1)} %get-tuple-element.52), custom_call_target="InvertDiagBlocksLowerTriangular" | custom-call | tf_op jit(solution)/shard_map/jit(cholesky)/cholesky | solution.py:18
  303.5 11.9 %custom-call.47 = f32[1,128,128]{2,1,0:T(8,128)S(1)} custom-call(f32[1,128,128]{2,1,0:T(8,128)S(1)} %cholesky.456), custom_call_target="Cholesky" | custom-call | tf_op jit(solution)/shard_map/jit(cholesky)/cholesky | solution.py:18
  316.8 9.8 %custom-call.48 = f32[1,1,128,128]{2,3,1,0:T(8,128)S(1)} custom-call(f32[1,1,128,128]{3,2,1,0:T(8,128)S(1)} %get-tuple-element.49), custom_call_target="InvertDiagBlocksLowerTriangular" | custom-call | tf_op jit(solution)/shard_map/jit(cholesky)/cholesky | solution.py:18
  327.1 11.7 %custom-call.49 = f32[1,128,128]{2,1,0:T(8,128)S(1)} custom-call(f32[1,128,128]{2,1,0:T(8,128)S(1)} %cholesky.461), custom_call_target="Cholesky" | custom-call | tf_op jit(solution)/shard_map/jit(cholesky)/cholesky | solution.py:18
  339.5 9.8 %custom-call.50 = f32[1,1,128,128]{2,3,1,0:T(8,128)S(1)} custom-call(f32[1,1,128,128]{3,2,1,0:T(8,128)S(1)} %get-tuple-element.46), custom_call_target="InvertDiagBlocksLowerTriangular" | custom-call | tf_op jit(solution)/shard_map/jit(cholesky)/cholesky | solution.py:18
  354.5 6.4 %while.5 = (s32[]{:T(128)}, f32[1,400,400]{2,1,0:T(8,128)S(1)}, s32[3,2]{0,1:T(2,128)S(1)}, f32[3,1,128,128]{3,2,1,0:T(8,128)S(1)}, s32[]{:T(128)}) while((s32[]{:T(128)}, f32[1,400,400]{2,1,0:T(8,128)S(1)}, s32[3,2]{0,1:T(2,128)S(1)}, f32[3,1,128,128]{3,2,1,0:T(8,128)S(1)}, s32[]{:T(128)}) %tuple.63), condition=%wide.while_cond.clone, body=%wide.while_body.clone.sunk | while | flops 2 | bytes 131181 | solution.py:21
  361.0 39.3 %custom-call.52 = f32[1,4,128,128]{2,3,1,0:T(8,128)S(1)} custom-call(f32[1,4,128,128]{3,2,1,0:T(8,128)S(1)} %pad_maximum_fusion.1), custom_call_target="InvertDiagBlocksLowerTriangular" | custom-call | tf_op jit(solution)/shard_map/vmap(jit(_cho_solve))/triangular_solve | solution.py:21
  (176 shorter events, 66.6 us)
Async XLA Ops:
  6.5 56.4 %reduce-scatter.3.cloned.1.call-start = ((), (), s32[]{:S(2)}) async-start(), calls=%async_computation.2 | async-start | bytes 3072000 | tf_op jit(solution)/shard_map/reduce_scatter | solution.py:63
  15.0 6.9 %copy-start.14 = (f32[2112]{0:T(1024)}, f32[2112]{0:T(1024)S(1)}, u32[]{:S(2)}) copy-start(f32[2112]{0:T(1024)S(1)} %convert_element_type.41) | copy-start | bytes 25348
  15.0 7.0 %copy-start = (bf16[4,2112,400]{1,2,0:T(8,128)(2,1)S(1)}, bf16[4,2112,400]{1,2,0:T(8,128)(2,1)}, u32[]{:S(2)}) copy-start(bf16[4,2112,400]{1,2,0:T(8,128)(2,1)} %param.15) | copy-start | bytes 20275204
  16.7 5.3 %copy-start.5 = (f32[2112,300]{0,1:T(8,128)}, f32[2112,300]{0,1:T(8,128)S(1)}, u32[]{:S(2)}) copy-start(f32[2112,300]{0,1:T(8,128)S(1)} %convert_element_type.43) | copy-start | bytes 7603204
  22.0 5.6 %copy-start.24 = (bf16[2112]{0:T(1024)(128)(2,1)S(1)}, bf16[2112]{0:T(1024)(128)(2,1)}, u32[]{:S(2)}) copy-start(bf16[2112]{0:T(1024)(128)(2,1)} %param.16) | copy-start | bytes 12676
  22.0 5.6 %copy-start.20 = (f32[300]{0:T(512)S(1)}, f32[300]{0:T(512)}, u32[]{:S(2)}) copy-start(f32[300]{0:T(512)} %param.19) | copy-start | bytes 3604
  22.1 6.2 %copy-start.25 = (u32[32]{0:T(128)S(1)}, u32[32]{0:T(128)}, u32[]{:S(2)}) copy-start(u32[32]{0:T(128)} %constant.174) | copy-start | bytes 388
  22.1 6.8 %copy-start.19 = (bf16[2112]{0:T(1024)(128)(2,1)S(1)}, bf16[2112]{0:T(1024)(128)(2,1)}, u32[]{:S(2)}) copy-start(bf16[2112]{0:T(1024)(128)(2,1)} %param.17) | copy-start | bytes 12676
  22.1 6.8 %copy-start.1 = (bf16[2112,300]{0,1:T(8,128)(2,1)S(1)}, bf16[2112,300]{0,1:T(8,128)(2,1)}, u32[]{:S(2)}) copy-start(bf16[2112,300]{0,1:T(8,128)(2,1)} %param.14) | copy-start | bytes 3801604
  22.1 6.8 %copy-start.16 = (bf16[4,2112]{1,0:T(4,128)(2,1)S(1)}, bf16[4,2112]{1,0:T(4,128)(2,1)}, u32[]{:S(2)}) copy-start(bf16[4,2112]{1,0:T(4,128)(2,1)} %param.13) | copy-start | bytes 50692
  22.1 40.8 %copy-start.18 = (f32[400]{0:T(512)S(1)}, f32[400]{0:T(512)}, u32[]{:S(2)}) copy-start(f32[400]{0:T(512)} %param.20) | copy-start | bytes 4804
  27.6 250.4 %reduce-scatter.5.cloned.1.call-start = ((), (), s32[]{:S(2)}) async-start(), calls=%async_computation.3 | async-start | bytes 3072000 | tf_op jit(solution)/shard_map/reduce_scatter | solution.py:63
  27.7 38.0 %copy-start.10 = (f32[2112]{0:T(1024)}, f32[2112]{0:T(1024)S(1)}, u32[]{:S(2)}) copy-start(f32[2112]{0:T(1024)S(1)} %convert_element_type.45) | copy-start | bytes 25348
  28.9 36.8 %copy-start.12 = (f32[2112]{0:T(1024)}, f32[2112]{0:T(1024)S(1)}, u32[]{:S(2)}) copy-start(f32[2112]{0:T(1024)S(1)} %broadcast_multiply_fusion) | copy-start | bytes 25348
  65.7 146.8 %copy-start.2 = (f32[1,300,400]{1,2,0:T(8,128)S(1)}, f32[1,300,400]{1,2,0:T(8,128)}, u32[]{:S(2)}) copy-start(f32[1,300,400]{1,2,0:T(8,128)} %reduce-scatter.3.cloned.1.call-done) | copy-start | bytes 1440004
  66.1 12.3 %copy-start.7 = (f32[1,400,400]{2,1,0:T(8,128)}, f32[1,400,400]{2,1,0:T(8,128)S(1)}, u32[]{:S(2)}) copy-start(f32[1,400,400]{2,1,0:T(8,128)S(1)} %fusion.43) | copy-start | bytes 1920004
  88.9 150.0 %slice-start = ((s8[6963200]{0:T(1024)(128)(4,1)}), s8[2768896]{0:T(1024)(128)(4,1)S(1)}, s32[]{:S(2)}) async-start(s8[6963200]{0:T(1024)(128)(4,1)} %bitcast.560), calls=%async_computation.4 | async-start | bytes 5537792
  93.0 0.6 copy-start.8
  122.2 0.6 copy-start.9
  158.0 1.4 copy-start.4
  158.0 80.8 %copy-start.15 = (f32[2112]{0:T(1024)S(1)}, f32[2112]{0:T(1024)}, u32[]{:S(2)}) copy-start(f32[2112]{0:T(1024)} %copy-done.14) | copy-start | bytes 25348
  212.5 26.4 %copy-start.6 = (f32[2112,300]{0,1:T(8,128)S(1)}, f32[2112,300]{0,1:T(8,128)}, u32[]{:S(2)}) copy-start(f32[2112,300]{0,1:T(8,128)} %copy-done.5) | copy-start | bytes 7603204
  218.8 20.0 %slice-start.1 = ((s8[6963200]{0:T(1024)(128)(4,1)}), s8[4194304]{0:T(1024)(128)(4,1)S(1)}, s32[]{:S(2)}) async-start(s8[6963200]{0:T(1024)(128)(4,1)} %bitcast.560), calls=%async_computation.5 | async-start | bytes 8388608
  238.9 5.5 %copy-start.11 = (f32[2112]{0:T(1024)S(1)}, f32[2112]{0:T(1024)}, u32[]{:S(2)}) copy-start(f32[2112]{0:T(1024)} %copy-done.10) | copy-start | bytes 25348
  238.9 5.5 %copy-start.13 = (f32[2112]{0:T(1024)S(1)}, f32[2112]{0:T(1024)}, u32[]{:S(2)}) copy-start(f32[2112]{0:T(1024)} %copy-done.12) | copy-start | bytes 25348
  238.9 5.5 %copy-start.17 = (bf16[4,2112]{1,0:T(4,128)(2,1)S(1)}, bf16[4,2112]{1,0:T(4,128)(2,1)}, u32[]{:S(2)}) copy-start(bf16[4,2112]{1,0:T(4,128)(2,1)} %param.13) | copy-start | bytes 50692
  238.9 39.1 %copy-start.21 = (f32[300]{0:T(512)S(1)}, f32[300]{0:T(512)}, u32[]{:S(2)}) copy-start(f32[300]{0:T(512)} %param.19) | copy-start | bytes 3604
  280.7 119.6 %copy-start.3 = (f32[1,300,400]{1,2,0:T(8,128)S(1)}, f32[1,300,400]{1,2,0:T(8,128)}, u32[]{:S(2)}) copy-start(f32[1,300,400]{1,2,0:T(8,128)} %reduce-scatter.5.cloned.1.call-done) | copy-start | bytes 1440004
  280.7 119.6 %copy-start.22 = (f32[1,300]{1,0:T(1,128)S(1)}, f32[1,300]{1,0:T(1,128)}, u32[]{:S(2)}) copy-start(f32[1,300]{1,0:T(1,128)} %broadcast_in_dim.9) | copy-start | bytes 3604
  280.7 119.6 %copy-start.23 = (f32[1,400]{1,0:T(1,128)S(1)}, f32[1,400]{1,0:T(1,128)}, u32[]{:S(2)}) copy-start(f32[1,400]{1,0:T(1,128)} %param.21) | copy-start | bytes 4804
Sparse Core Ops, SparseCore 0:
  27.7 35.1 reduce-scatter.2
  244.5 33.3 reduce-scatter.4
where the time goes:
time: 418 us; the launch traced here: 412 us
  other arithmetic  235 us (56%)
  matrix products  58.2 us (14%)
  waiting for transfers between devices  50.2 us (12%)
  blocking collectives  25.9 us (6%)
  local copies, waits for them, and re-layouts  23.2 us (6%)
  between operations  19.3 us (5%)
    another operation x29, other arithmetic, solve_step(): factor = jnp.linalg.cholesky(normal)  145 us
    another operation x11, other arithmetic, one_solve(): return jax.scipy.linalg.cho_solve((fac, True), vec)  83.8 us
    reduce_scatter x2, waiting for transfers between devices, local(): lax.psum_scatter(pc_jacob, 'chan', scatter_dimension=0, tiled=True)  50.2 us
    another operation x23, local copies, waits for them, and re-layouts, one_solve(): return jax.scipy.linalg.cho_solve((fac, True), vec)  18 us
    another operation x28, matrix products, one_solve(): return jax.scipy.linalg.cho_solve((fac, True), vec)  16.8 us
    unnamed x2, blocking collectives  14.5 us
    all_gather x2, blocking collectives, local(): lax.all_gather(states.astype(jnp.bfloat16), 'chan', axis=0, tiled=True)  11.4 us
    dot_general x2, matrix products, project(): jnp.einsum('rck,rcs->rks', weighted, jacobian, preferred_element_type=jnp...  10.9 us
  transfers between devices with their start and end apart: 2, of which 2 were waited for; matrix products, arithmetic and copies ran while one was open for 1% of the time, Pallas kernels for 0%

commit v1 on v0

--- a/solution.py
+++ b/solution.py
@@ -1,27 +1,119 @@
-import jax
-import jax.numpy as jnp
+import functools
+import jax, jax.numpy as jnp
 from jax import lax
+from jax.experimental import pallas as pl
+from jax.experimental.pallas import tpu as pltpu
+
 from jax.sharding import PartitionSpec as P
 
 ITERS = 2
+HI = lax.Precision.HIGHEST
+TILE, LANES = 8, 128
 
 
-def solve_step(states, pc_resid, pc_jacob, pc_weight, prior_prec, prior_mean):
-    highest = lax.Precision.HIGHEST
-    weighted_jac = pc_jacob * pc_weight[None, :, None]
-    normal = jnp.einsum("rks,rkt->rst", weighted_jac, pc_jacob, precision=highest)
-    normal = (
-        normal + jnp.eye(pc_jacob.shape[2], dtype=jnp.float32)[None] * prior_prec[None, None, :]
-    )
-    gradient = jnp.einsum("rks,rk->rs", pc_jacob, pc_weight[None, :] * pc_resid, precision=highest)
-    gradient = gradient + prior_prec[None, :] * (states - prior_mean)
-    factor = jnp.linalg.cholesky(normal)
+def up(n, m):
+    return -(-n // m) * m
 
-    def one_solve(fac, vec):
-        return jax.scipy.linalg.cho_solve((fac, True), vec)
 
-    update = jax.vmap(one_solve)(factor, gradient)
-    return states - update
+def eliminate(mat, first, rows, width):
+    tiles = rows // TILE
+    spans = (width - first) // LANES
+    sub = lax.broadcasted_iota(jnp.int32, (TILE, LANES), 0)
+
+    def group(q, carry):
+        base = pl.multiple_of(first + q * TILE, TILE)
+        piv = [mat[pl.ds(base, TILE), first + w * LANES:first + (w + 1) * LANES] for w in range(spans)]
+
+        def spread(tile, k):
+            where = jnp.full((TILE, LANES), q * TILE + k, jnp.int32)
+            return jnp.take_along_axis(tile, where, axis=1, mode="promise_in_bounds")
+
+        cols = [spread(piv[0], k) for k in range(TILE)]
+        for t in range(TILE):
+            inv = 1.0 / jnp.broadcast_to(cols[t][t:t + 1], (TILE, LANES))
+            at = sub == t
+            factor = jnp.where(at, 1.0 - inv, cols[t] * inv)
+            cols = [c if k <= t else c - factor * jnp.broadcast_to(c[t:t + 1], (TILE, LANES)) for k, c in enumerate(cols)]
+            piv = [c - factor * jnp.broadcast_to(c[t:t + 1], (TILE, LANES)) for c in piv]
+        lines = [[jnp.broadcast_to(c[k:k + 1], (TILE, LANES)) for k in range(TILE)] for c in piv]
+        for i in range(tiles):
+            at = slice(first + i * TILE, first + (i + 1) * TILE)
+            old = [mat[at, first + w * LANES:first + (w + 1) * LANES] for w in range(spans)]
+            mult = [spread(old[0], k) for k in range(TILE)]
+            for w in range(spans):
+                acc = [mult[k] * lines[w][k] for k in range(TILE)]
+                while len(acc) > 1:
+                    acc = [acc[2 * z] + acc[2 * z + 1] for z in range(len(acc) // 2)]
+                mat[at, first + w * LANES:first + (w + 1) * LANES] = old[w] - acc[0]
+        for w in range(spans):
+            mat[pl.ds(base, TILE), first + w * LANES:first + (w + 1) * LANES] = piv[w]
+        return carry
+
+    lax.fori_loop(0, tiles, group, 0)
+
+
+def solver_kernel(jac_ref, resid_ref, weight_ref, prec_ref, mean_ref, state_ref, out_ref, aug, mat, held):
+    count, size = jac_ref.shape
+    rows, lanes = mat.shape
+    root = jnp.sqrt(prec_ref[...])
+    aug[...] = jnp.zeros_like(aug)
+    jac = jac_ref[...] * (1.0 / root)
+    aug[0:count, :] = jac
+    aug[rows:rows + 1, :] = (state_ref[...] - mean_ref[...]) * root
+    full = lax.dot_general(aug[0:rows, :], aug[...], (((1,), (1,)), ((), ())), precision=HI, preferred_element_type=jnp.float32)
+    r = lax.broadcasted_iota(jnp.int32, full.shape, 0)
+    c = lax.broadcasted_iota(jnp.int32, full.shape, 1)
+    mat[...] = full + jnp.where(r == c, 1.0 / weight_ref[...], 0.0) - jnp.where(c == rows, resid_ref[...], 0.0)
+    for first in range(0, rows, LANES):
+        here = min(LANES, rows - first)
+        after = first + here
+        if after < rows:
+            held[0:here, 0:lanes - after] = mat[first:after, after:lanes]
+        eliminate(mat, first, here, lanes)
+        if after < rows:
+            mat[after:rows, after:lanes] = mat[after:rows, after:lanes] - lax.dot_general(
+                held[0:here, 0:rows - after], mat[first:after, after:lanes], (((0,), (0,)), ((), ())),
+                precision=HI, preferred_element_type=jnp.float32)
+    out_ref[...] = back(mat, aug, rows, lanes, mean_ref, root)
+
+
+def back(mat, aug, rows, lanes, mean_ref, root):
+    total = None
+    solved = []
+    start = (rows - 1) // LANES * LANES
+    for first in range(start, -1, -LANES):
+        here = min(LANES, rows - first)
+        z = mat[first:first + here, rows:rows + 1]
+        for at, width, later in solved:
+            z = z - jnp.sum(mat[first:first + here, at:at + width] * later, axis=1, keepdims=True)
+        part = jnp.sum(aug[first:first + here, :] * z, axis=0, keepdims=True)
+        total = part if total is None else total + part
+        if first > 0:
+            flat = jnp.transpose(jnp.broadcast_to(z, (here, LANES)))[0:1, :]
+            solved.append((first, here, flat))
+    return mean_ref[...] + total / root
+
+
+def solve(states, resid, jac, weight, prec, mean):
+    count, size = jac.shape
+    rows = up(count, TILE)
+    lanes = up(rows + 1, LANES)
+    wide = lanes
+    weight = jnp.pad(weight, (0, rows - count), constant_values=1.0)[:, None]
+    resid = jnp.pad(resid, ((0, rows - count), (0, 0)))
+    vmem = pl.BlockSpec(memory_space=pltpu.VMEM)
+    return pl.pallas_call(
+        solver_kernel,
+        out_shape=jax.ShapeDtypeStruct((1, size), jnp.float32),
+        in_specs=[vmem] * 6,
+        out_specs=vmem,
+        scratch_shapes=[
+            pltpu.VMEM((wide, size), jnp.float32),
+            pltpu.VMEM((rows, lanes), jnp.float32),
+            pltpu.VMEM((LANES, lanes), jnp.float32),
+        ],
+        compiler_params=pltpu.CompilerParams(vmem_limit_bytes=32 * 2**20),
+    )(jac, resid, weight, prec[None, :], mean, states)
 
 
 def project(state_bf, spectra, valid, eigvec, jacobian, radiance_base, curvature):
@@ -62,7 +154,11 @@
             lax.psum_scatter(pc_resid, "chan", scatter_dimension=0, tiled=True),
             lax.psum_scatter(pc_jacob, "chan", scatter_dimension=0, tiled=True),
         )
-        states = solve_step(states, pc_resid, pc_jacob, pc_weight, prior_prec, prior_mean)
+        own = [
+            solve(states[p:p + 1], pc_resid[p][:, None], pc_jacob[p], pc_weight, prior_prec, prior_mean[p:p + 1])
+            for p in range(states.shape[0])
+        ]
+        states = own[0] if len(own) == 1 else jnp.concatenate(own, axis=0)
     return states
 
 

time: 418 us -> 160 us (0.38); the launches traced: 412 us -> 160 us
  other arithmetic: 235 us -> 4.9 us
  Pallas kernels: 0 us -> 37.9 us
  matrix products: 58.2 us -> 21 us
  local copies, waits for them, and re-layouts: 23.2 us -> 4.77 us
  between operations: 19.3 us -> 13.7 us
    another operation x40 -> x0, other arithmetic: 229 us -> none  [the longest x29 145 us: solve_step(): factor = jnp.linalg.cholesky(normal)]
    pallas_call x0 -> x2, Pallas kernels: none -> 37.9 us  [solve(): pl.pallas_call(solver_kernel, out_shape=jax.ShapeDtypeStruct((1, size), j...]
    another operation x40 -> x0, matrix products: 26.9 us -> none  [the longest x28 16.8 us: one_solve(): return jax.scipy.linalg.cho_solve((fac, True), vec)]
    another operation x31 -> x4, local copies, waits for them, and re-layouts: 19.7 us -> 1.59 us  [local(): pc_resid[p][:, None]]
    dot_general x4 -> x0, matrix products: 8.92 us -> none  [the longest x2 5.46 us: solve_step(): jnp.einsum('rks,rkt->rst', weighted_jac, pc_jacob, precision=highest)]
  transfers between devices with their start and end apart: 2 -> 2, of which waited for: 2 -> 2; matrix products, arithmetic and copies ran while one was open for 1% -> 2% of each run, Pallas kernels for 0% -> 0%
where the time goes in v1:
time: 160 us
  waiting for transfers between devices  51.9 us (32%)
  Pallas kernels  37.9 us (24%)
  blocking collectives  25.3 us (16%)
  matrix products  21 us (13%)
  between operations  13.7 us (9%)
  other arithmetic  4.9 us (3%)
  local copies, waits for them, and re-layouts  4.77 us (3%)
    reduce_scatter x2, waiting for transfers between devices, local(): lax.psum_scatter(pc_jacob, 'chan', scatter_dimension=0, tiled=True)  51.9 us
    pallas_call x2, Pallas kernels, solve(): pl.pallas_call(solver_kernel, out_shape=jax.ShapeDtypeStruct((1, size), j...  37.9 us
    unnamed x2, blocking collectives  14 us
    dot_general x2, matrix products, project(): jnp.einsum('rck,rcs->rks', weighted, jacobian, preferred_element_type=jnp...  12.1 us
    all_gather x2, blocking collectives, local(): lax.all_gather(states.astype(jnp.bfloat16), 'chan', axis=0, tiled=True)  11.4 us
    dot_general x2, matrix products, project(): jnp.einsum('rs,rcs->rc', state_bf, jacobian, preferred_element_type=jnp.f...  8 us
  transfers between devices with their start and end apart: 2, of which 2 were waited for; matrix products, arithmetic and copies ran while one was open for 2% of the time, Pallas kernels for 0%

profile of v1, /device:TPU:0, one launch (start us, length us, event | category | flops | bytes accessed | tf_op | source)
XLA Modules:
  0.0 159.6 jit_solution(15461642254097929389)
XLA Ops:
  6.5 0.7 convert_element_type.41
  7.2 0.1 broadcast_in_dim.6
  7.3 0.2 reshape.10
  7.5 1.6 %convert_element_type.44 = f32[2112,300]{0,1:T(8,128)S(1)} convert(bf16[2112,300]{0,1:T(8,128)(2,1)} %param.11) | non-fusion elementwise | flops 633600 | bytes 3801600 | tf_op jit(solution)/shard_map/convert_element_type | solution.py:127
  9.1 1.8 %convert_bitcast_fusion.1 = bf16[1,1,400]{2,1,0:T(2,128)(2,1)S(1)} fusion(f32[1,400]{1,0:T(1,128)} %state_ref.1), kind=kLoop, calls=%fused_computation.38 | loop fusion | flops 400 | bytes 2400
  10.9 6.2 %all-gather = bf16[4,1,400]{2,1,0:T(2,128)(2,1)S(1)} all-gather(bf16[1,1,400]{2,1,0:T(2,128)(2,1)S(1)} %convert_bitcast_fusion.1), channel_id=1, replica_groups=mesh['chan'=4,'prof'=8] {'chan'}, dimensions={0}, use_global_device_ids=true | all-gather | bytes 4000 | tf_op jit(solution)/shard_map/all_gather | solution.py:149
  17.1 0.7 convert_element_type.42
  17.8 4.0 %fusion.26 = f32[4,1,2112]{2,1,0:T(1,128)S(1)} fusion(bf16[4,2112,400]{1,2,0:T(8,128)(2,1)} %param.12, bf16[4,1,400]{2,1,0:T(2,128)(2,1)S(1)} %all-gather), kind=kOutput, calls=%fused_computation.34 | convolution fusion | flops 6758400 | bytes 6795392 | tf_op jit(solution)/shard_map/rs,rcs->rc/dot_general | solution.py:122
  21.9 0.0 copy-start.13
  22.0 4.5 %fusion = f32[4,300,400]{2,1,0:T(8,128)} fusion(bf16[4,2112,400]{1,2,0:T(8,128)(2,1)S(1)} %copy-done.5, f32[2112,300]{0,1:T(8,128)S(1)} %convert_element_type.44, f32[4,2112]{1,0:T(4,128)S(1)} %fusion.15), kind=kOutput, calls=%fused_computation.2 | convolution fusion | flops 2032588800 | bytes 11246592 | tf_op jit(solution)/shard_map/rck,rcs->rks/dot_general | solution.py:129
  26.5 0.0 reduce-scatter.3.cloned.1.call-update
  26.5 0.0 reduce-scatter.5.cloned.1.call-start
  26.6 0.6 dynamic-slice
  27.2 0.4 fusion.18
  27.7 7.7 %all-reduce.3 = f32[4,300]{1,0:T(4,128)S(1)} all-reduce(f32[4,300]{1,0:T(4,128)S(1)} %fusion.18), channel_id=3, replica_groups=mesh['chan'=4,'prof'=8] {'chan'}, use_global_device_ids=true, to_apply=%region_1.0.clone | all-reduce | flops 1200 | bytes 9600
  35.4 0.7 dynamic-slice_bitcast_fusion.1
  36.1 0.1 copy.20
  36.2 0.1 broadcast_in_dim.9.weight_ref
  36.4 25.7 %reduce-scatter.3.cloned.1.call-done = f32[1,300,400]{2,1,0:T(8,128)} async-done(((f32[4,300,400]{2,1,0:T(8,128)}), f32[1,300,400]{2,1,0:T(8,128)}) %reduce-scatter.3.cloned.1.call-update) | async-done | bytes 480016 | tf_op jit(solution)/shard_map/reduce_scatter | solution.py:155
  62.1 1.1 copy-done
  63.1 18.6 %shard_map.100.state_ref = f32[1,400]{1,0:T(1,128)S(1)} custom-call(f32[300,400]{1,0:T(8,128)S(1)} %bitcast.46, f32[304,1]{1,0:T(8,128)S(1)} %pad.12.resid_ref, f32[304,1]{1,0:T(8,128)S(1)} %broadcast_in_dim.9.weight_ref, f32[1,400]{1,0:T(1,128)S(1)} %bitcast.48, f32[1,400]{1,0:T(1,128)S(1)} %copy-done.3, f32[1,400]{1,0:T(1,128)S(1)} %copy-done.4), custom_call_target="tpu_custom_call" | custom-call | tf_op jit(solution)/shard_map/pallas_call | solution.py:105
  81.8 5.2 %all-gather.1 = bf16[4,1,400]{2,1,0:T(2,128)(2,1)S(1)} all-gather(bf16[1,1,400]{2,1,0:T(2,128)(2,1)S(1)} %convert_bitcast_fusion), channel_id=1, replica_groups=mesh['chan'=4,'prof'=8] {'chan'}, dimensions={0}, use_global_device_ids=true | all-gather | bytes 4000 | tf_op jit(solution)/shard_map/all_gather | solution.py:149
  87.0 4.0 %fusion.24 = f32[4,1,2112]{2,1,0:T(1,128)S(1)} fusion(bf16[4,2112,400]{1,2,0:T(8,128)(2,1)} %param.12, bf16[4,1,400]{2,1,0:T(2,128)(2,1)S(1)} %all-gather.1), kind=kOutput, calls=%fused_computation.32 | convolution fusion | flops 6758400 | bytes 6795392 | tf_op jit(solution)/shard_map/rs,rcs->rc/dot_general | solution.py:122
  91.0 7.6 %fusion.1 = f32[4,300,400]{2,1,0:T(8,128)} fusion(bf16[4,2112,400]{1,2,0:T(8,128)(2,1)} %param.12, f32[4,2112]{1,0:T(4,128)S(1)} %fusion.13, f32[2112,300]{0,1:T(8,128)S(1)} %copy-done.8), kind=kOutput, calls=%fused_computation.3 | convolution fusion | flops 2032588800 | bytes 11246592 | tf_op jit(solution)/shard_map/rck,rcs->rks/dot_general | solution.py:129
  98.6 0.0 reduce-scatter.5.cloned.1.call-update
  98.6 0.4 fusion.16
  99.1 6.3 %all-reduce.4 = f32[4,300]{1,0:T(4,128)S(1)} all-reduce(f32[4,300]{1,0:T(4,128)S(1)} %fusion.16), channel_id=5, replica_groups=mesh['chan'=4,'prof'=8] {'chan'}, use_global_device_ids=true, to_apply=%region_3.4.clone | all-reduce | flops 1200 | bytes 9600
  105.4 0.7 dynamic-slice_bitcast_fusion
  106.0 0.1 copy.23
  106.2 26.2 %reduce-scatter.5.cloned.1.call-done = f32[1,300,400]{2,1,0:T(8,128)} async-done(((f32[4,300,400]{2,1,0:T(8,128)}), f32[1,300,400]{2,1,0:T(8,128)}) %reduce-scatter.5.cloned.1.call-update) | async-done | bytes 480016 | tf_op jit(solution)/shard_map/reduce_scatter | solution.py:155
  132.4 1.1 copy-done.1
  133.5 19.2 %shard_map.101 = f32[1,400]{1,0:T(1,128)} custom-call(f32[300,400]{1,0:T(8,128)S(1)} %bitcast.47, f32[304,1]{1,0:T(8,128)S(1)} %pad.14.resid_ref, f32[304,1]{1,0:T(8,128)S(1)} %broadcast_in_dim.9.weight_ref, f32[1,400]{1,0:T(1,128)S(1)} %bitcast.49, f32[1,400]{1,0:T(1,128)S(1)} %copy-done.3, f32[1,400]{1,0:T(1,128)S(1)} %shard_map.100.state_ref), custom_call_target="tpu_custom_call" | custom-call | tf_op jit(solution)/shard_map/pallas_call | solution.py:105
  (34 shorter events, 0.2 us)
Async XLA Ops:
  6.5 55.5 %reduce-scatter.3.cloned.1.call-start = ((), (), s32[]{:S(2)}) async-start(), calls=%async_computation.2 | async-start | bytes 3112960 | tf_op jit(solution)/shard_map/reduce_scatter | solution.py:155
  7.5 14.4 %copy-start.5 = (bf16[4,2112,400]{1,2,0:T(8,128)(2,1)S(1)}, bf16[4,2112,400]{1,2,0:T(8,128)(2,1)}, u32[]{:S(2)}) copy-start(bf16[4,2112,400]{1,2,0:T(8,128)(2,1)} %param.12) | copy-start | bytes 20275204
  9.1 12.7 %copy-start.7 = (f32[2112,300]{0,1:T(8,128)}, f32[2112,300]{0,1:T(8,128)S(1)}, u32[]{:S(2)}) copy-start(f32[2112,300]{0,1:T(8,128)S(1)} %convert_element_type.44) | copy-start | bytes 7603204
  21.9 4.7 %copy-start.11 = (bf16[2112]{0:T(1024)(128)(2,1)S(1)}, bf16[2112]{0:T(1024)(128)(2,1)}, u32[]{:S(2)}) copy-start(bf16[2112]{0:T(1024)(128)(2,1)} %param.13) | copy-start | bytes 12676
  21.9 4.7 %copy-start.13 = (u32[32]{0:T(128)S(1)}, u32[32]{0:T(128)}, u32[]{:S(2)}) copy-start(u32[32]{0:T(128)} %constant.21) | copy-start | bytes 388
  21.9 5.3 %copy-start.10 = (bf16[2112]{0:T(1024)(128)(2,1)S(1)}, bf16[2112]{0:T(1024)(128)(2,1)}, u32[]{:S(2)}) copy-start(bf16[2112]{0:T(1024)(128)(2,1)} %param.14) | copy-start | bytes 12676
  21.9 5.3 %copy-start.6 = (bf16[2112,300]{0,1:T(8,128)(2,1)S(1)}, bf16[2112,300]{0,1:T(8,128)(2,1)}, u32[]{:S(2)}) copy-start(bf16[2112,300]{0,1:T(8,128)(2,1)} %param.11) | copy-start | bytes 3801604
  21.9 5.3 %copy-start.9 = (bf16[4,2112]{1,0:T(4,128)(2,1)S(1)}, bf16[4,2112]{1,0:T(4,128)(2,1)}, u32[]{:S(2)}) copy-start(bf16[4,2112]{1,0:T(4,128)(2,1)} %param.10) | copy-start | bytes 50692
  21.9 14.3 %copy-start.12 = (f32[300]{0:T(512)S(1)}, f32[300]{0:T(512)}, u32[]{:S(2)}) copy-start(f32[300]{0:T(512)} %param.16) | copy-start | bytes 3604
  22.0 40.1 %copy-start.2 = (f32[400]{0:T(512)S(1)}, f32[400]{0:T(512)}, u32[]{:S(2)}) copy-start(f32[400]{0:T(512)} %param.17) | copy-start | bytes 4804
  22.0 40.1 %copy-start.3 = (f32[1,400]{1,0:T(1,128)S(1)}, f32[1,400]{1,0:T(1,128)}, u32[]{:S(2)}) copy-start(f32[1,400]{1,0:T(1,128)} %mean_ref.3) | copy-start | bytes 4804
  22.0 40.1 %copy-start.4 = (f32[1,400]{1,0:T(1,128)S(1)}, f32[1,400]{1,0:T(1,128)}, u32[]{:S(2)}) copy-start(f32[1,400]{1,0:T(1,128)} %state_ref.1) | copy-start | bytes 4804
  26.5 105.9 %reduce-scatter.5.cloned.1.call-start = ((), (), s32[]{:S(2)}) async-start(), calls=%async_computation.3 | async-start | bytes 3112960 | tf_op jit(solution)/shard_map/reduce_scatter | solution.py:155
  62.0 1.1 copy-start
  63.1 27.9 %copy-start.8 = (f32[2112,300]{0,1:T(8,128)S(1)}, f32[2112,300]{0,1:T(8,128)}, u32[]{:S(2)}) copy-start(f32[2112,300]{0,1:T(8,128)} %copy-done.7) | copy-start | bytes 7603204
  132.4 1.1 copy-start.1
Sparse Core Ops, SparseCore 0:
  26.7 35.3 reduce-scatter.2
  98.7 33.6 reduce-scatter.4

commit v2 on v1

--- a/solution.py
+++ b/solution.py
@@ -9,6 +9,7 @@
 ITERS = 2
 HI = lax.Precision.HIGHEST
 TILE, LANES = 8, 128
+MESH = pl.DeviceIdType.MESH
 
 
 def up(n, m):
@@ -63,7 +64,11 @@
     full = lax.dot_general(aug[0:rows, :], aug[...], (((1,), (1,)), ((), ())), precision=HI, preferred_element_type=jnp.float32)
     r = lax.broadcasted_iota(jnp.int32, full.shape, 0)
     c = lax.broadcasted_iota(jnp.int32, full.shape, 1)
-    mat[...] = full + jnp.where(r == c, 1.0 / weight_ref[...], 0.0) - jnp.where(c == rows, resid_ref[...], 0.0)
+    mat[...] = full + jnp.where(r == c, 1.0 / weight_ref[...], 0.0)
+    for first in range(0, rows, LANES):
+        here = min(LANES, rows - first)
+        column = jnp.transpose(jnp.broadcast_to(resid_ref[:, first:first + LANES], (LANES, LANES)))[0:here, 0:1]
+        mat[first:first + here, rows:rows + 1] = mat[first:first + here, rows:rows + 1] - column
     for first in range(0, rows, LANES):
         here = min(LANES, rows - first)
         after = first + here
@@ -100,7 +105,7 @@
     lanes = up(rows + 1, LANES)
     wide = lanes
     weight = jnp.pad(weight, (0, rows - count), constant_values=1.0)[:, None]
-    resid = jnp.pad(resid, ((0, rows - count), (0, 0)))
+    resid = jnp.pad(resid, ((0, 0), (0, lanes - count)))
     vmem = pl.BlockSpec(memory_space=pltpu.VMEM)
     return pl.pallas_call(
         solver_kernel,
@@ -116,18 +121,106 @@
     )(jac, resid, weight, prec[None, :], mean, states)
 
 
-def project(state_bf, spectra, valid, eigvec, jacobian, radiance_base, curvature):
-    shift_f = radiance_base.astype(jnp.float32)
-    curve_f = curvature.astype(jnp.float32)
-    linear = jnp.einsum("rs,rcs->rc", state_bf, jacobian, preferred_element_type=jnp.float32)
-    misfit = (
-        valid * (shift_f + linear + 0.5 * curve_f * linear * linear - spectra.astype(jnp.float32))
-    ).astype(jnp.bfloat16)
-    slope = valid * (1.0 + curve_f * linear)
-    weighted = (slope[:, :, None] * eigvec[None]).astype(jnp.bfloat16)
-    pc_resid = jnp.dot(misfit, eigvec, preferred_element_type=jnp.float32)
-    pc_jacob = jnp.einsum("rck,rcs->rks", weighted, jacobian, preferred_element_type=jnp.float32)
-    return (pc_resid, pc_jacob)
+def partner(me, m, n):
+    out, bit = 0, 1
+    while bit < n:
+        out = out + ((me // bit + (m // bit) % 2) % 2) * bit
+        bit *= 2
+    return out
+
+
+def project_kernel(
+    n, state_ref, jac_ref, eig_ref, valid_ref, base_ref, curve_ref, jac_out, resid_out,
+    slabs, states, mis, weighted, sent, came, rows_out, rows_in,
+    slab_sem, state_send, state_recv, jac_send, jac_recv, row_send, row_recv,
+):
+    me = lax.axis_index("chan")
+    order = list(range(n - 1, 0, -1)) + [0]
+    loads = {}
+    for m in order:
+        q = partner(me, m, n)
+        loads[m] = pltpu.make_async_copy(jac_ref.at[q], slabs.at[m], slab_sem.at[m])
+        loads[m].start()
+    barrier = pltpu.get_barrier_semaphore()
+    for m in range(1, n):
+        pl.semaphore_signal(barrier, inc=1, device_id={"chan": partner(me, m, n)}, device_id_type=MESH)
+    pl.semaphore_wait(barrier, n - 1)
+
+    def send(src, dst, ssem, rsem, m):
+        copy = pltpu.make_async_remote_copy(
+            src_ref=src, dst_ref=dst, send_sem=ssem.at[m], recv_sem=rsem.at[m],
+            device_id={"chan": partner(me, m, n)}, device_id_type=MESH)
+        copy.start()
+        return copy
+
+    state_copies = {m: send(state_ref, states.at[m], state_send, state_recv, m) for m in range(1, n)}
+    curve = curve_ref[...]
+    row_copies, jac_copies = {}, {}
+    for m in order:
+        q = partner(me, m, n)
+        if m:
+            state_copies[m].wait_recv()
+            state = states[m]
+        else:
+            state = state_ref[...]
+        loads[m].wait()
+        state = jnp.broadcast_to(state, (16, state.shape[1])).astype(jnp.bfloat16)
+        linear = jnp.dot(state, slabs[m], preferred_element_type=jnp.float32)[0:8]
+        valid = valid_ref[q]
+        misfit = valid * (base_ref[q] + linear + 0.5 * curve * linear * linear)
+        mis[m] = misfit[0:1]
+        slope = valid * (1.0 + curve * linear)
+        weighted[...] = (slope[0:1] * eig_ref[...].astype(jnp.float32)).astype(jnp.bfloat16)
+        if m == 0:
+            every = jnp.concatenate([mis[z] for z in range(n)] + [jnp.zeros_like(mis[0])] * (up(n, 16) - n), axis=0).astype(jnp.bfloat16)
+            project = lax.dot_general(every, eig_ref[...], (((1,), (1,)), ((), ())), preferred_element_type=jnp.float32)
+            for z in range(n):
+                rows_out[z] = project[z:z + 1]
+            for z in range(1, n):
+                row_copies[z] = send(rows_out.at[z], rows_in.at[z], row_send, row_recv, z)
+        part = lax.dot_general(weighted[...], slabs[m], (((1,), (1,)), ((), ())), preferred_element_type=jnp.float32)
+        if m:
+            sent[m] = part.astype(jnp.bfloat16)
+            jac_copies[m] = send(sent.at[m], came.at[m], jac_send, jac_recv, m)
+        else:
+            jac_out[...] = part
+    resid = rows_out[0]
+    for m in order[:-1]:
+        row_copies[m].wait_recv()
+        resid = resid + rows_in[m]
+    resid_out[...] = resid
+    for m in order[:-1]:
+        jac_copies[m].wait_recv()
+        jac_out[...] += came[m].astype(jnp.float32)
+    for m in range(1, n):
+        state_copies[m].wait_send()
+        row_copies[m].wait_send()
+        jac_copies[m].wait_send()
+
+
+def project(index, n, state, jac, eig, valid, base, curve):
+    comps, chans = eig.shape
+    size = jac.shape[1]
+    vmem = pl.BlockSpec(memory_space=pltpu.VMEM)
+    dma = pltpu.SemaphoreType.DMA((n,))
+    return pl.pallas_call(
+        functools.partial(project_kernel, n),
+        out_shape=(jax.ShapeDtypeStruct((comps, size), jnp.float32), jax.ShapeDtypeStruct((1, comps), jnp.float32)),
+        in_specs=[vmem, pl.BlockSpec(memory_space=pl.ANY), vmem, vmem, vmem, vmem],
+        out_specs=(vmem, vmem),
+        scratch_shapes=[
+            pltpu.VMEM((n, size, chans), jnp.bfloat16),
+            pltpu.VMEM((n, 1, size), jnp.float32),
+            pltpu.VMEM((n, 1, chans), jnp.float32),
+            pltpu.VMEM((comps, chans), jnp.bfloat16),
+            pltpu.VMEM((n, comps, size), jnp.bfloat16),
+            pltpu.VMEM((n, comps, size), jnp.bfloat16),
+            pltpu.VMEM((n, 1, comps), jnp.float32),
+            pltpu.VMEM((n, 1, comps), jnp.float32),
+        ] + [dma] * 7,
+        compiler_params=pltpu.CompilerParams(
+            collective_id=index, has_side_effects=True, vmem_limit_bytes=48 * 2**20),
+    )(state, jac, eig, valid, base, curve)
 
 
 def local(
@@ -141,30 +234,24 @@
     prior_prec,
     prior_mean,
     state0,
+    n,
 ):
     block_width = observed.shape[1] // block_mask.shape[1]
     states = state0
-    valid = jnp.repeat(block_mask.astype(jnp.float32), block_width, axis=1)
+    valid = jnp.repeat(block_mask.astype(jnp.float32), block_width, axis=1)[:, None, :]
+    base = (radiance_base.astype(jnp.float32)[None] - observed.astype(jnp.float32))[:, None, :]
+    curve = curvature.astype(jnp.float32)[None]
+    eig = eigvec.T
+    jac = jnp.swapaxes(jacobian, 1, 2)
     for iteration in range(ITERS):
-        state_bf = lax.all_gather(states.astype(jnp.bfloat16), "chan", axis=0, tiled=True)
-        pc_resid, pc_jacob = project(
-            state_bf, observed, valid, eigvec, jacobian, radiance_base, curvature
-        )
-        pc_resid, pc_jacob = (
-            lax.psum_scatter(pc_resid, "chan", scatter_dimension=0, tiled=True),
-            lax.psum_scatter(pc_jacob, "chan", scatter_dimension=0, tiled=True),
-        )
-        own = [
-            solve(states[p:p + 1], pc_resid[p][:, None], pc_jacob[p], pc_weight, prior_prec, prior_mean[p:p + 1])
-            for p in range(states.shape[0])
-        ]
-        states = own[0] if len(own) == 1 else jnp.concatenate(own, axis=0)
+        pc_jacob, pc_resid = project(iteration, n, states, jac, eig, valid, base, curve)
+        states = solve(states, pc_resid, pc_jacob, pc_weight, prior_prec, prior_mean)
     return states
 
 
 def solution(mesh):
     return jax.shard_map(
-        local,
+        functools.partial(local, n=mesh.shape["chan"]),
         mesh=mesh,
         in_specs=(
             P("prof", "chan"),

time: 160 us -> 87.2 us (0.55)
  waiting for transfers between devices: 51.9 us -> 0 us
  Pallas kernels: 37.9 us -> 80.8 us
  blocking collectives: 25.3 us -> 0 us
  matrix products: 21 us -> 0 us
  between operations: 13.7 us -> 0.11 us
  other arithmetic: 4.9 us -> 2.15 us
    reduce_scatter x2 -> x0, waiting for transfers between devices: 51.9 us -> none  [local(): lax.psum_scatter(pc_jacob, 'chan', scatter_dimension=0, tiled=True)]
    pallas_call x0 -> x2, Pallas kernels: none -> 42.8 us  [project(): pl.pallas_call(functools.partial(project_kernel, n), out_shape=(jax.Shape...]
    dot_general x6 -> x0, matrix products: 21 us -> none  [the longest x2 12.1 us: project(): jnp.einsum('rck,rcs->rks', weighted, jacobian, preferred_element_type=jnp...]
    unnamed x2 -> x0, blocking collectives: 14 us -> none
    all_gather x2 -> x0, blocking collectives: 11.4 us -> none  [local(): lax.all_gather(states.astype(jnp.bfloat16), 'chan', axis=0, tiled=True)]
    unnamed x2 -> x0, other arithmetic: 1.81 us -> none
    convert_element_type x4 -> x2, other arithmetic: 3.03 us -> 1.42 us  [the longest x1 0.72 us: local(): block_mask.astype(jnp.float32)]
  transfers between devices with their start and end apart: 2 -> 0, of which waited for: 2 -> 0; matrix products, arithmetic and copies ran while one was open for 2% -> 0% of each run, Pallas kernels for 0% -> 0%
where the time goes in v2:
time: 87.2 us; the launch traced here: 86.9 us
  Pallas kernels  80.8 us (93%)
  local copies, waits for them, and re-layouts  3.79 us (4%)
  other arithmetic  2.15 us (2%)
    pallas_call x2, Pallas kernels, project(): pl.pallas_call(functools.partial(project_kernel, n), out_shape=(jax.Shape...  42.8 us
    pallas_call x2, Pallas kernels, solve(): pl.pallas_call(solver_kernel, out_shape=jax.ShapeDtypeStruct((1, size), j...  38.1 us
    unnamed x12, local copies, waits for them, and re-layouts  2.02 us

profile of v2, /device:TPU:0, one launch (start us, length us, event | category | flops | bytes accessed | tf_op | source)
XLA Modules:
  0.0 86.9 jit_solution(15709522584432283241)
XLA Ops:
  0.0 0.0 copy-start.5
  0.0 0.0 copy-start.3
  0.0 0.0 copy-start.2
  0.0 0.7 convert_element_type.13
  0.7 0.7 pad.13
  1.4 0.7 reshape.1.curve_ref
  2.1 0.7 convert_element_type.14
  2.8 0.7 convert_subtract_fusion
  3.6 0.1 broadcast_in_dim.20
  3.7 0.2 broadcast_in_dim_reshape.4.valid_ref
  3.9 0.1 broadcast_in_dim.27.weight_ref
  4.0 0.0 copy-start
  4.0 1.3 %copy-done = bf16[2112,300]{0,1:T(8,128)(2,1)S(1)} copy-done((bf16[2112,300]{0,1:T(8,128)(2,1)S(1)}, bf16[2112,300]{0,1:T(8,128)(2,1)}, u32[]{:S(2)}) %copy-start) | copy-done | bytes 1267224
  5.3 0.0 copy-start.4
  5.3 0.7 copy-done.4
  6.0 0.0 copy-start.1
  6.0 22.8 %shard_map.100 = (f32[300,400]{1,0:T(8,128)S(1)}, f32[1,300]{1,0:T(1,128)S(1)}) custom-call(f32[1,400]{1,0:T(1,128)S(1)} %copy-done.4, bf16[4,400,2112]{2,1,0:T(8,128)(2,1)} %bitcast.7, bf16[300,2112]{1,0:T(8,128)(2,1)S(1)} %bitcast.3, f32[4,1,2112]{2,1,0:T(1,128)S(1)} %broadcast_in_dim_reshape.4.valid_ref, f32[4,1,2112]{2,1,0:T(1,128)S(1)} %broadcast_in_dim.21.base_ref, ...), custom_call_target="tpu_custom_call" | custom-call | tf_op jit(solution)/shard_map/pallas_call | solution.py:206
  28.8 0.0 copy-done.5
  28.8 0.0 copy-done.3
  28.8 0.0 copy-done.2
  28.8 18.8 %shard_map.101.state_ref = f32[1,400]{1,0:T(1,128)S(1)} custom-call(f32[300,400]{1,0:T(8,128)S(1)} %get-tuple-element.9.jac_ref, f32[1,384]{1,0:T(1,128)S(1)} %pad.12.resid_ref, f32[304,1]{1,0:T(8,128)S(1)} %broadcast_in_dim.27.weight_ref, f32[1,400]{1,0:T(1,128)S(1)} %bitcast.5, f32[1,400]{1,0:T(1,128)S(1)} %copy-done.3, f32[1,400]{1,0:T(1,128)S(1)} %copy-done.5), custom_call_target="tpu_custom_call" | custom-call | tf_op jit(solution)/shard_map/pallas_call | solution.py:110
  47.7 0.0 copy-done.1
  47.7 20.0 %shard_map.102 = (f32[300,400]{1,0:T(8,128)S(1)}, f32[1,300]{1,0:T(1,128)S(1)}) custom-call(f32[1,400]{1,0:T(1,128)S(1)} %shard_map.101.state_ref, bf16[4,400,2112]{2,1,0:T(8,128)(2,1)} %bitcast.8, bf16[300,2112]{1,0:T(8,128)(2,1)S(1)} %bitcast.4, f32[4,1,2112]{2,1,0:T(1,128)S(1)} %broadcast_in_dim_reshape.4.valid_ref, ...), custom_call_target="tpu_custom_call" | custom-call | tf_op jit(solution)/shard_map/pallas_call | solution.py:206
  67.6 19.2 %shard_map.103 = f32[1,400]{1,0:T(1,128)} custom-call(f32[300,400]{1,0:T(8,128)S(1)} %get-tuple-element.11.jac_ref, f32[1,384]{1,0:T(1,128)S(1)} %pad.14.resid_ref, f32[304,1]{1,0:T(8,128)S(1)} %broadcast_in_dim.27.weight_ref, f32[1,400]{1,0:T(1,128)S(1)} %bitcast.6, f32[1,400]{1,0:T(1,128)S(1)} %copy-done.3, f32[1,400]{1,0:T(1,128)S(1)} %shard_map.101.state_ref), custom_call_target="tpu_custom_call" | custom-call | tf_op jit(solution)/shard_map/pallas_call | solution.py:110
  (3 shorter events, 0.0 us)
Async XLA Ops:
  0.0 28.8 %copy-start.5 = (f32[1,400]{1,0:T(1,128)S(1)}, f32[1,400]{1,0:T(1,128)}, u32[]{:S(2)}) copy-start(f32[1,400]{1,0:T(1,128)} %state_ref.3) | copy-start | bytes 4804
  0.0 28.8 %copy-start.3 = (f32[1,400]{1,0:T(1,128)S(1)}, f32[1,400]{1,0:T(1,128)}, u32[]{:S(2)}) copy-start(f32[1,400]{1,0:T(1,128)} %mean_ref.3) | copy-start | bytes 4804
  0.0 28.8 %copy-start.2 = (f32[400]{0:T(512)S(1)}, f32[400]{0:T(512)}, u32[]{:S(2)}) copy-start(f32[400]{0:T(512)} %param.17) | copy-start | bytes 4804
  4.0 1.3 %copy-start = (bf16[2112,300]{0,1:T(8,128)(2,1)S(1)}, bf16[2112,300]{0,1:T(8,128)(2,1)}, u32[]{:S(2)}) copy-start(bf16[2112,300]{0,1:T(8,128)(2,1)} %param.11) | copy-start | bytes 3801604
  5.3 0.7 copy-start.4
  6.0 41.7 %copy-start.1 = (bf16[2112,300]{0,1:T(8,128)(2,1)S(1)}, bf16[2112,300]{0,1:T(8,128)(2,1)}, u32[]{:S(2)}) copy-start(bf16[2112,300]{0,1:T(8,128)(2,1)} %param.11) | copy-start | bytes 3801604

commit v3 on v2

--- a/solution.py
+++ b/solution.py
@@ -7,8 +7,8 @@
 from jax.sharding import PartitionSpec as P
 
 ITERS = 2
-HI = lax.Precision.HIGHEST
 TILE, LANES = 8, 128
+BLOCK = 32
 MESH = pl.DeviceIdType.MESH
 
 
@@ -16,17 +16,29 @@
     return -(-n // m) * m
 
 
+def split(x):
+    high = x.astype(jnp.bfloat16)
+    return high, (x - high.astype(jnp.float32)).astype(jnp.bfloat16)
+
+
+def product(a, b, dims):
+    (ah, al), (bh, bl) = split(a), split(b)
+    dot = functools.partial(lax.dot_general, dimension_numbers=(dims, ((), ())), preferred_element_type=jnp.float32)
+    return dot(ah, bh) + (dot(ah, bl) + dot(al, bh))
+
+
 def eliminate(mat, first, rows, width):
     tiles = rows // TILE
-    spans = (width - first) // LANES
+    left = first // LANES * LANES
+    spans = (width - left) // LANES
     sub = lax.broadcasted_iota(jnp.int32, (TILE, LANES), 0)
 
     def group(q, carry):
         base = pl.multiple_of(first + q * TILE, TILE)
-        piv = [mat[pl.ds(base, TILE), first + w * LANES:first + (w + 1) * LANES] for w in range(spans)]
+        piv = [mat[pl.ds(base, TILE), left + w * LANES:left + (w + 1) * LANES] for w in range(spans)]
 
         def spread(tile, k):
-            where = jnp.full((TILE, LANES), q * TILE + k, jnp.int32)
+            where = jnp.full((TILE, LANES), first - left + q * TILE + k, jnp.int32)
             return jnp.take_along_axis(tile, where, axis=1, mode="promise_in_bounds")
 
         cols = [spread(piv[0], k) for k in range(TILE)]
@@ -39,15 +51,15 @@
         lines = [[jnp.broadcast_to(c[k:k + 1], (TILE, LANES)) for k in range(TILE)] for c in piv]
         for i in range(tiles):
             at = slice(first + i * TILE, first + (i + 1) * TILE)
-            old = [mat[at, first + w * LANES:first + (w + 1) * LANES] for w in range(spans)]
+            old = [mat[at, left + w * LANES:left + (w + 1) * LANES] for w in range(spans)]
             mult = [spread(old[0], k) for k in range(TILE)]
             for w in range(spans):
                 acc = [mult[k] * lines[w][k] for k in range(TILE)]
                 while len(acc) > 1:
                     acc = [acc[2 * z] + acc[2 * z + 1] for z in range(len(acc) // 2)]
-                mat[at, first + w * LANES:first + (w + 1) * LANES] = old[w] - acc[0]
+                mat[at, left + w * LANES:left + (w + 1) * LANES] = old[w] - acc[0]
         for w in range(spans):
-            mat[pl.ds(base, TILE), first + w * LANES:first + (w + 1) * LANES] = piv[w]
+            mat[pl.ds(base, TILE), left + w * LANES:left + (w + 1) * LANES] = piv[w]
         return carry
 
     lax.fori_loop(0, tiles, group, 0)
@@ -61,7 +73,7 @@
     jac = jac_ref[...] * (1.0 / root)
     aug[0:count, :] = jac
     aug[rows:rows + 1, :] = (state_ref[...] - mean_ref[...]) * root
-    full = lax.dot_general(aug[0:rows, :], aug[...], (((1,), (1,)), ((), ())), precision=HI, preferred_element_type=jnp.float32)
+    full = product(aug[0:rows, :], aug[...], ((1,), (1,)))
     r = lax.broadcasted_iota(jnp.int32, full.shape, 0)
     c = lax.broadcasted_iota(jnp.int32, full.shape, 1)
     mat[...] = full + jnp.where(r == c, 1.0 / weight_ref[...], 0.0)
@@ -69,33 +81,30 @@
         here = min(LANES, rows - first)
         column = jnp.transpose(jnp.broadcast_to(resid_ref[:, first:first + LANES], (LANES, LANES)))[0:here, 0:1]
         mat[first:first + here, rows:rows + 1] = mat[first:first + here, rows:rows + 1] - column
-    for first in range(0, rows, LANES):
-        here = min(LANES, rows - first)
+    for first in range(0, rows, BLOCK):
+        here = min(BLOCK, rows - first)
         after = first + here
+        left = after // LANES * LANES
         if after < rows:
-            held[0:here, 0:lanes - after] = mat[first:after, after:lanes]
+            held[0:here, 0:lanes - left] = mat[first:after, left:lanes]
         eliminate(mat, first, here, lanes)
         if after < rows:
-            mat[after:rows, after:lanes] = mat[after:rows, after:lanes] - lax.dot_general(
-                held[0:here, 0:rows - after], mat[first:after, after:lanes], (((0,), (0,)), ((), ())),
-                precision=HI, preferred_element_type=jnp.float32)
+            change = product(held[0:here, 0:rows - left], mat[first:after, left:lanes], ((0,), (0,)))
+            mat[after:rows, left:lanes] = mat[after:rows, left:lanes] - change[after - left:]
     out_ref[...] = back(mat, aug, rows, lanes, mean_ref, root)
 
 
 def back(mat, aug, rows, lanes, mean_ref, root):
     total = None
-    solved = []
-    start = (rows - 1) // LANES * LANES
-    for first in range(start, -1, -LANES):
-        here = min(LANES, rows - first)
-        z = mat[first:first + here, rows:rows + 1]
-        for at, width, later in solved:
-            z = z - jnp.sum(mat[first:first + here, at:at + width] * later, axis=1, keepdims=True)
+    solved = jnp.zeros((1, lanes), jnp.float32)
+    for first in range((rows - 1) // BLOCK * BLOCK, -1, -BLOCK):
+        here = min(BLOCK, rows - first)
+        z = mat[first:first + here, rows:rows + 1] - jnp.sum(mat[first:first + here, :] * solved, axis=1, keepdims=True)
         part = jnp.sum(aug[first:first + here, :] * z, axis=0, keepdims=True)
         total = part if total is None else total + part
-        if first > 0:
-            flat = jnp.transpose(jnp.broadcast_to(z, (here, LANES)))[0:1, :]
-            solved.append((first, here, flat))
+        r = lax.broadcasted_iota(jnp.int32, (here, lanes), 0)
+        c = lax.broadcasted_iota(jnp.int32, (here, lanes), 1)
+        solved = solved + jnp.sum(jnp.where(r + first == c, z, 0.0), axis=0, keepdims=True)
     return mean_ref[...] + total / root
 
 

time: 87.2 us -> 74.8 us (0.86)
  Pallas kernels: 80.8 us -> 68.4 us
    pallas_call x2, Pallas kernels: 38.1 us -> 25.6 us  [solve(): pl.pallas_call(solver_kernel, out_shape=jax.ShapeDtypeStruct((1, size), j...]
where the time goes in v3:
time: 74.8 us; the launch traced here: 74.4 us
  Pallas kernels  68.4 us (91%)
  local copies, waits for them, and re-layouts  3.79 us (5%)
  other arithmetic  2.15 us (3%)
    pallas_call x2, Pallas kernels, project(): pl.pallas_call(functools.partial(project_kernel, n), out_shape=(jax.Shape...  42.8 us
    pallas_call x2, Pallas kernels, solve(): pl.pallas_call(solver_kernel, out_shape=jax.ShapeDtypeStruct((1, size), j...  25.6 us
    unnamed x12, local copies, waits for them, and re-layouts  2.02 us

profile of v3, /device:TPU:0, one launch (start us, length us, event | category | flops | bytes accessed | tf_op | source)
XLA Modules:
  0.0 74.4 jit_solution(8370027667635942293)
XLA Ops:
  0.0 0.0 copy-start.5
  0.0 0.0 copy-start.3
  0.0 0.0 copy-start.2
  0.0 0.7 convert_element_type.13
  0.7 0.7 pad.13
  1.4 0.7 reshape.1.curve_ref
  2.1 0.7 convert_element_type.14
  2.8 0.7 convert_subtract_fusion
  3.6 0.1 broadcast_in_dim.20
  3.7 0.2 broadcast_in_dim_reshape.4.valid_ref
  3.9 0.1 broadcast_in_dim.27.weight_ref
  4.0 0.0 copy-start
  4.0 1.3 %copy-done = bf16[2112,300]{0,1:T(8,128)(2,1)S(1)} copy-done((bf16[2112,300]{0,1:T(8,128)(2,1)S(1)}, bf16[2112,300]{0,1:T(8,128)(2,1)}, u32[]{:S(2)}) %copy-start) | copy-done | bytes 1267224
  5.3 0.0 copy-start.4
  5.3 0.7 copy-done.4
  6.0 0.0 copy-start.1
  6.0 22.8 %shard_map.100 = (f32[300,400]{1,0:T(8,128)S(1)}, f32[1,300]{1,0:T(1,128)S(1)}) custom-call(f32[1,400]{1,0:T(1,128)S(1)} %copy-done.4, bf16[4,400,2112]{2,1,0:T(8,128)(2,1)} %bitcast.7, bf16[300,2112]{1,0:T(8,128)(2,1)S(1)} %bitcast.3, f32[4,1,2112]{2,1,0:T(1,128)S(1)} %broadcast_in_dim_reshape.4.valid_ref, f32[4,1,2112]{2,1,0:T(1,128)S(1)} %broadcast_in_dim.21.base_ref, ...), custom_call_target="tpu_custom_call" | custom-call | tf_op jit(solution)/shard_map/pallas_call | solution.py:215
  28.8 0.0 copy-done.5
  28.8 0.0 copy-done.3
  28.8 0.0 copy-done.2
  28.8 12.6 %shard_map.101.state_ref = f32[1,400]{1,0:T(1,128)S(1)} custom-call(f32[300,400]{1,0:T(8,128)S(1)} %get-tuple-element.9.jac_ref, f32[1,384]{1,0:T(1,128)S(1)} %pad.12.resid_ref, f32[304,1]{1,0:T(8,128)S(1)} %broadcast_in_dim.27.weight_ref, f32[1,400]{1,0:T(1,128)S(1)} %bitcast.5, f32[1,400]{1,0:T(1,128)S(1)} %copy-done.3, f32[1,400]{1,0:T(1,128)S(1)} %copy-done.5), custom_call_target="tpu_custom_call" | custom-call | tf_op jit(solution)/shard_map/pallas_call | solution.py:119
  41.4 0.0 copy-done.1
  41.4 20.0 %shard_map.102 = (f32[300,400]{1,0:T(8,128)S(1)}, f32[1,300]{1,0:T(1,128)S(1)}) custom-call(f32[1,400]{1,0:T(1,128)S(1)} %shard_map.101.state_ref, bf16[4,400,2112]{2,1,0:T(8,128)(2,1)} %bitcast.8, bf16[300,2112]{1,0:T(8,128)(2,1)S(1)} %bitcast.4, f32[4,1,2112]{2,1,0:T(1,128)S(1)} %broadcast_in_dim_reshape.4.valid_ref, ...), custom_call_target="tpu_custom_call" | custom-call | tf_op jit(solution)/shard_map/pallas_call | solution.py:215
  61.4 13.0 %shard_map.103 = f32[1,400]{1,0:T(1,128)} custom-call(f32[300,400]{1,0:T(8,128)S(1)} %get-tuple-element.11.jac_ref, f32[1,384]{1,0:T(1,128)S(1)} %pad.14.resid_ref, f32[304,1]{1,0:T(8,128)S(1)} %broadcast_in_dim.27.weight_ref, f32[1,400]{1,0:T(1,128)S(1)} %bitcast.6, f32[1,400]{1,0:T(1,128)S(1)} %copy-done.3, f32[1,400]{1,0:T(1,128)S(1)} %shard_map.101.state_ref), custom_call_target="tpu_custom_call" | custom-call | tf_op jit(solution)/shard_map/pallas_call | solution.py:119
  (3 shorter events, 0.0 us)
Async XLA Ops:
  0.0 28.8 %copy-start.5 = (f32[1,400]{1,0:T(1,128)S(1)}, f32[1,400]{1,0:T(1,128)}, u32[]{:S(2)}) copy-start(f32[1,400]{1,0:T(1,128)} %state_ref.3) | copy-start | bytes 4804
  0.0 28.8 %copy-start.3 = (f32[1,400]{1,0:T(1,128)S(1)}, f32[1,400]{1,0:T(1,128)}, u32[]{:S(2)}) copy-start(f32[1,400]{1,0:T(1,128)} %mean_ref.3) | copy-start | bytes 4804
  0.0 28.8 %copy-start.2 = (f32[400]{0:T(512)S(1)}, f32[400]{0:T(512)}, u32[]{:S(2)}) copy-start(f32[400]{0:T(512)} %param.17) | copy-start | bytes 4804
  4.0 1.3 %copy-start = (bf16[2112,300]{0,1:T(8,128)(2,1)S(1)}, bf16[2112,300]{0,1:T(8,128)(2,1)}, u32[]{:S(2)}) copy-start(bf16[2112,300]{0,1:T(8,128)(2,1)} %param.11) | copy-start | bytes 3801604
  5.3 0.7 copy-start.4
  6.0 35.5 %copy-start.1 = (bf16[2112,300]{0,1:T(8,128)(2,1)S(1)}, bf16[2112,300]{0,1:T(8,128)(2,1)}, u32[]{:S(2)}) copy-start(bf16[2112,300]{0,1:T(8,128)(2,1)} %param.11) | copy-start | bytes 3801604
